TPU v7x, 32 devices: a whole 2x2x4 slice. The times are simulated.
32 devices in a mesh: group: 4 (over z), replica: 8 (over y, x, core).
Axes of the slice: x: 2, y: 2, z: 4, core: 2. Of those that a mesh axis runs over, the one named last changes fastest.
Arguments:
- layer_input: bfloat16 [8, 1024, 2560], P('replica', 'group')
- positions: int32 [8, 1024], P('replica', 'group'), may hold values from 0 to 543, as said below
- piece_starts: int32 [8, 2], P('replica'), may hold values from 0 to 768, as said below
- gain_attn: bfloat16 [2560], P('group'), may hold values from 0.5 to 1.5
- w_query: bfloat16 [2560, 2560], P('group'), may hold values from -0.125 to 0.125
- w_key: bfloat16 [2560, 640], P('group'), may hold values from -0.125 to 0.125
- w_value: bfloat16 [2560, 640], P('group'), may hold values from -0.125 to 0.125
- w_out: bfloat16 [2560, 2560], P('group'), may hold values from -2 to 2
- gain_mlp: bfloat16 [2560], P('group'), may hold values from 0.5 to 1.5
- w_gate: bfloat16 [2560, 7168], P('group'), may hold values from -0.125 to 0.125
- w_up: bfloat16 [2560, 7168], P('group'), may hold values from -0.125 to 0.125
- w_down: bfloat16 [2560, 7168], P('group'), may hold values from -0.0625 to 0.0625
- out_grad: bfloat16 [8, 1024, 2560], P('replica', 'group'), may hold values from -6 to 6
Outputs:
- layer_out: bfloat16 [8, 1024, 2560], P('replica', 'group')
- input_grad: float32 [8, 1024, 2560], P('replica', 'group')
- grad_norm_attn: float32 [2560], P(('group', 'replica'))
- grad_query: float32 [2560, 2560], P(('group', 'replica'))
- grad_key: float32 [2560, 640], P(('group', 'replica'))
- grad_value: float32 [2560, 640], P(('group', 'replica'))
- grad_out: float32 [2560, 2560], P(('group', 'replica'))
- grad_norm_mlp: float32 [2560], P(('group', 'replica'))
- grad_gate: float32 [2560, 7168], P(('group', 'replica'))
- grad_up: float32 [2560, 7168], P(('group', 'replica'))
- grad_down: float32 [2560, 7168], P(('group', 'replica'))
- stream_rms: float32 [8, 3], P('replica')
Inputs may be any that keep to these rules, and one draw needn't show every extreme that they name: `piece_starts`: each sequence holds two picture pieces of 256 tokens that start at multiples of 128, the second starting 256 or more tokens after the first, both ending inside the sequence. `positions`: outside picture pieces a token's position is one more than the previous token's; the j-th token of a piece whose first token has position p gets p + j // 16, and the token after the piece gets p + 16; a sequence's first token has position 0.
All inputs are finite; a program needn't handle non-finite values.
Results may differ from a plain program's by a relative error of at most 0.018.
Values may be sent and summed in bfloat16 or wider, within the bound.
No kernel may reach another device: no remote copies, remote signals or barrier semaphores. Data moves between devices by JAX's collectives and lax.ppermute only.
A program may use at most 384 MiB of HBM per device.

v0:
```python
import jax
import jax.numpy as jnp
from jax import lax
from jax.sharding import PartitionSpec as P

HEADS = 32
KV_HEADS = 8
HEAD_DIM = 80
PIECE = 256
epsilon = 1e-05
rope_base = 1000000.0


def rope_tables(places):
    halves = HEAD_DIM // 2
    frequency = rope_base ** (-(jnp.arange(halves, dtype=jnp.float32) * 2.0 / HEAD_DIM))
    angles = places.astype(jnp.float32)[..., None] * frequency
    angles = jnp.concatenate([angles, angles], axis=-1)
    return (jnp.cos(angles), jnp.sin(angles))


def rotate(values, cosine, sine):
    halves = HEAD_DIM // 2
    turned = jnp.concatenate([-values[..., halves:], values[..., :halves]], axis=-1)
    return values * cosine[:, :, None, :] + turned * sine[:, :, None, :]


def unrotate(grads, cosine, sine):
    halves = HEAD_DIM // 2
    shifted = grads * sine[:, :, None, :]
    turned = jnp.concatenate([shifted[..., halves:], -shifted[..., :halves]], axis=-1)
    return grads * cosine[:, :, None, :] + turned


def times_t(left, right):
    return lax.dot_general(
        left, right, (((1,), (1,)), ((), ())), preferred_element_type=jnp.float32
    )


def inner_t(left, right):
    return lax.dot_general(
        left, right, (((0,), (0,)), ((), ())), preferred_element_type=jnp.float32
    )


def inverse_rms(values):
    return lax.rsqrt(jnp.mean(values * values, axis=-1, keepdims=True) + epsilon)


def norm_back(grad_normed, source, inverse, gain_full):
    weighted = grad_normed * gain_full
    average = jnp.mean(weighted * source, axis=-1, keepdims=True)
    return inverse * weighted - source * (inverse * inverse * inverse) * average


def piece_index(starts, places):
    labels = jnp.zeros(places.shape, jnp.int32)
    for which in range(2):
        inside = (places >= starts[which]) & (places < starts[which] + PIECE)
        labels = jnp.where(inside, which + 1, labels)
    return labels


def shards(
    layer_input,
    positions,
    piece_starts,
    gain_attn,
    w_query,
    w_key,
    w_value,
    w_out,
    gain_mlp,
    w_gate,
    w_up,
    w_down,
    out_grad,
):
    sequences, block_size, model_width = layer_input.shape
    token_rows = sequences * block_size
    kv_width = KV_HEADS * HEAD_DIM
    repeats = HEADS // KV_HEADS
    scaling = HEAD_DIM ** (-0.5)
    full_len = block_size * lax.axis_size("group")
    source = layer_input.astype(jnp.float32).reshape(token_rows, model_width)
    inverse_one = inverse_rms(source)
    unit_one = source * inverse_one
    gain_piece = lax.all_gather(gain_attn, "group", axis=0, tiled=True)
    query_piece = lax.all_gather(w_query, "group", axis=0, tiled=True)
    key_piece = lax.all_gather(w_key, "group", axis=0, tiled=True)
    value_piece = lax.all_gather(w_value, "group", axis=0, tiled=True)
    out_piece = lax.all_gather(w_out, "group", axis=0, tiled=True)
    scaled = unit_one * gain_piece.astype(jnp.float32)
    scaled = scaled.astype(jnp.bfloat16)
    query = jnp.dot(scaled, query_piece, preferred_element_type=jnp.float32)
    keyed = jnp.dot(scaled, key_piece, preferred_element_type=jnp.float32)
    valued = jnp.dot(scaled, value_piece, preferred_element_type=jnp.float32)
    normed = scaled
    gains = gain_piece
    out_full = out_piece
    query_lin, key_lin, value_lin, normed_one, gain_one_low, out_full = (
        query,
        keyed,
        valued,
        normed,
        gains,
        out_full,
    )
    gain_one = gain_one_low.astype(jnp.float32)
    cosine, sine = rope_tables(positions)
    query_rot = rotate(
        query_lin.reshape(sequences, block_size, HEADS, HEAD_DIM), cosine, sine
    ).astype(jnp.bfloat16)
    key_rot = rotate(
        key_lin.reshape(sequences, block_size, KV_HEADS, HEAD_DIM), cosine, sine
    ).astype(jnp.bfloat16)
    key_rot = key_rot.reshape(sequences, block_size, kv_width)
    value_low = value_lin.astype(jnp.bfloat16).reshape(sequences, block_size, kv_width)
    key_all, value_all = (
        lax.all_gather(key_rot, "group", axis=1, tiled=True),
        lax.all_gather(value_low, "group", axis=1, tiled=True),
    )
    query_places = lax.axis_index("group") * block_size + jnp.arange(block_size, dtype=jnp.int32)
    key_places = jnp.arange(full_len, dtype=jnp.int32)

    def allowed_for(starts):
        query_labels = piece_index(starts, query_places)
        key_labels = piece_index(starts, key_places)
        causal = key_places[None, :] <= query_places[:, None]
        same_piece = (query_labels[:, None] == key_labels[None, :]) & (query_labels[:, None] > 0)
        return causal | same_piece

    def scores_of(query_seq, key_seq, starts):
        grouped = query_seq.reshape(block_size, KV_HEADS, repeats, HEAD_DIM)
        keys_grouped = key_seq.reshape(full_len, KV_HEADS, HEAD_DIM)
        raw = (
            jnp.einsum("qkrd,skd->krqs", grouped, keys_grouped, preferred_element_type=jnp.float32)
            * scaling
        )
        return jnp.where(allowed_for(starts)[None, None], raw, -1e30)

    def attend_one(packed):
        query_seq, key_seq, value_seq, starts = packed
        masked = scores_of(query_seq, key_seq, starts)
        highest_score = jnp.max(masked, axis=-1, keepdims=True)
        raised = jnp.exp(masked - highest_score)
        summed = jnp.sum(raised, axis=-1, keepdims=True)
        chances_low = (raised / summed).astype(jnp.bfloat16)
        values_grouped = value_seq.reshape(full_len, KV_HEADS, HEAD_DIM)
        mixed = jnp.einsum(
            "krqs,skd->qkrd", chances_low, values_grouped, preferred_element_type=jnp.float32
        )
        return (mixed.reshape(block_size, model_width), highest_score + jnp.log(summed))

    mixed_all, log_totals = lax.map(attend_one, (query_rot, key_all, value_all, piece_starts))
    mixed_low = mixed_all.reshape(token_rows, model_width).astype(jnp.bfloat16)
    middle = source + times_t(mixed_low, out_full)
    inverse_two = inverse_rms(middle)
    unit_two = middle * inverse_two
    gain_piece = lax.all_gather(gain_mlp, "group", axis=0, tiled=True)
    gate_piece = lax.all_gather(w_gate, "group", axis=0, tiled=True)
    up_piece = lax.all_gather(w_up, "group", axis=0, tiled=True)
    down_piece = lax.all_gather(w_down, "group", axis=0, tiled=True)
    scaled = unit_two * gain_piece.astype(jnp.float32)
    scaled = scaled.astype(jnp.bfloat16)
    gated = jnp.dot(scaled, gate_piece, preferred_element_type=jnp.float32)
    lifted = jnp.dot(scaled, up_piece, preferred_element_type=jnp.float32)
    normed = scaled
    gains = gain_piece
    down_full = down_piece
    gated, lifted, normed_two, gain_two_low, down_full = (gated, lifted, normed, gains, down_full)
    gain_two = gain_two_low.astype(jnp.float32)
    activated = jax.nn.silu(gated)
    hidden = (activated * lifted).astype(jnp.bfloat16)
    output_full = middle + times_t(hidden, down_full)
    grad_low = out_grad.reshape(token_rows, model_width)
    grad_top = grad_low.astype(jnp.float32)
    grad_hidden = jnp.dot(grad_low, down_full, preferred_element_type=jnp.float32)
    sigmoid_gate = jax.nn.sigmoid(gated)
    grad_gate_low = (
        grad_hidden * lifted * (sigmoid_gate + gated * sigmoid_gate * (1.0 - sigmoid_gate))
    ).astype(jnp.bfloat16)
    grad_lift_low = (grad_hidden * activated).astype(jnp.bfloat16)
    gate_piece = lax.all_gather(w_gate, "group", axis=0, tiled=True)
    up_piece = lax.all_gather(w_up, "group", axis=0, tiled=True)
    added = times_t(grad_gate_low, gate_piece) + times_t(grad_lift_low, up_piece)
    grad_normed_two = added
    grad_gain_two = jnp.sum(grad_normed_two * unit_two, axis=0)
    grad_middle = grad_top + norm_back(grad_normed_two, middle, inverse_two, gain_two)
    grad_middle_low = grad_middle.astype(jnp.bfloat16)
    grad_mixed_low = jnp.dot(grad_middle_low, out_full, preferred_element_type=jnp.float32).astype(
        jnp.bfloat16
    )

    def attend_back(packed):
        query_seq, key_seq, value_seq, starts, log_total, grad_seq = packed
        masked = scores_of(query_seq, key_seq, starts)
        chances = jnp.exp(masked - log_total)
        grad_grouped = grad_seq.reshape(block_size, KV_HEADS, repeats, HEAD_DIM)
        values_grouped = value_seq.reshape(full_len, KV_HEADS, HEAD_DIM)
        keys_grouped = key_seq.reshape(full_len, KV_HEADS, HEAD_DIM)
        query_grouped = query_seq.reshape(block_size, KV_HEADS, repeats, HEAD_DIM)
        grad_value_seq = jnp.einsum(
            "krqs,qkrd->skd",
            chances.astype(jnp.bfloat16),
            grad_grouped,
            preferred_element_type=jnp.float32,
        )
        grad_chance = jnp.einsum(
            "qkrd,skd->krqs", grad_grouped, values_grouped, preferred_element_type=jnp.float32
        )
        grad_score = chances * (
            grad_chance - jnp.sum(chances * grad_chance, axis=-1, keepdims=True)
        )
        grad_score = grad_score.astype(jnp.bfloat16)
        grad_query_seq = (
            jnp.einsum(
                "krqs,skd->qkrd", grad_score, keys_grouped, preferred_element_type=jnp.float32
            )
            * scaling
        )
        grad_key_seq = (
            jnp.einsum(
                "krqs,qkrd->skd", grad_score, query_grouped, preferred_element_type=jnp.float32
            )
            * scaling
        )
        return (
            grad_query_seq.reshape(block_size, HEADS, HEAD_DIM),
            grad_key_seq.reshape(full_len, kv_width),
            grad_value_seq.reshape(full_len, kv_width),
        )

    grad_query_rot, grad_key_full, grad_value_full = lax.map(
        attend_back,
        (
            query_rot,
            key_all,
            value_all,
            piece_starts,
            log_totals,
            grad_mixed_low.reshape(sequences, block_size, model_width),
        ),
    )
    grad_key_rot, grad_value_sum = (
        lax.psum_scatter(grad_key_full, "group", scatter_dimension=1, tiled=True),
        lax.psum_scatter(grad_value_full, "group", scatter_dimension=1, tiled=True),
    )
    grad_query_low = (
        unrotate(grad_query_rot, cosine, sine).astype(jnp.bfloat16).reshape(token_rows, model_width)
    )
    grad_key_low = (
        unrotate(grad_key_rot.reshape(sequences, block_size, KV_HEADS, HEAD_DIM), cosine, sine)
        .astype(jnp.bfloat16)
        .reshape(token_rows, kv_width)
    )
    grad_value_low = grad_value_sum.astype(jnp.bfloat16).reshape(token_rows, kv_width)
    query_piece = lax.all_gather(w_query, "group", axis=0, tiled=True)
    key_piece = lax.all_gather(w_key, "group", axis=0, tiled=True)
    value_piece = lax.all_gather(w_value, "group", axis=0, tiled=True)
    added = (
        times_t(grad_query_low, query_piece)
        + times_t(grad_key_low, key_piece)
        + times_t(grad_value_low, value_piece)
    )
    grad_gain_one = jnp.sum(added * unit_one, axis=0)
    input_grad = grad_middle + norm_back(added, source, inverse_one, gain_one)
    normed_own, middle_own, normed_mlp_own, top_own = (
        lax.all_to_all(normed_one, "group", split_axis=1, concat_axis=0, tiled=True),
        lax.all_to_all(grad_middle_low, "group", split_axis=1, concat_axis=0, tiled=True),
        lax.all_to_all(normed_two, "group", split_axis=1, concat_axis=0, tiled=True),
        lax.all_to_all(grad_low, "group", split_axis=1, concat_axis=0, tiled=True),
    )
    query_rows, key_rows, value_rows, mixed_rows = (
        lax.all_gather(grad_query_low, "group", axis=0, tiled=True),
        lax.all_gather(grad_key_low, "group", axis=0, tiled=True),
        lax.all_gather(grad_value_low, "group", axis=0, tiled=True),
        lax.all_gather(mixed_low, "group", axis=0, tiled=True),
    )
    gate_rows, lift_rows, hidden_rows = (
        lax.all_gather(grad_gate_low, "group", axis=0, tiled=True),
        lax.all_gather(grad_lift_low, "group", axis=0, tiled=True),
        lax.all_gather(hidden, "group", axis=0, tiled=True),
    )
    partial_sums = (
        inner_t(normed_own, query_rows),
        inner_t(normed_own, key_rows),
        inner_t(normed_own, value_rows),
        inner_t(middle_own, mixed_rows),
        inner_t(normed_mlp_own, gate_rows),
        inner_t(normed_mlp_own, lift_rows),
        inner_t(top_own, hidden_rows),
    )
    grad_query, grad_key, grad_value, grad_out, grad_gate, grad_up, grad_down = (
        lax.psum_scatter(
            partial_sums[0].astype(jnp.bfloat16), "replica", scatter_dimension=0, tiled=True
        ).astype(jnp.float32),
        lax.psum_scatter(
            partial_sums[1].astype(jnp.bfloat16), "replica", scatter_dimension=0, tiled=True
        ).astype(jnp.float32),
        lax.psum_scatter(
            partial_sums[2].astype(jnp.bfloat16), "replica", scatter_dimension=0, tiled=True
        ).astype(jnp.float32),
        lax.psum_scatter(
            partial_sums[3].astype(jnp.bfloat16), "replica", scatter_dimension=0, tiled=True
        ).astype(jnp.float32),
        lax.psum_scatter(
            partial_sums[4].astype(jnp.bfloat16), "replica", scatter_dimension=0, tiled=True
        ).astype(jnp.float32),
        lax.psum_scatter(
            partial_sums[5].astype(jnp.bfloat16), "replica", scatter_dimension=0, tiled=True
        ).astype(jnp.float32),
        lax.psum_scatter(
            partial_sums[6].astype(jnp.bfloat16), "replica", scatter_dimension=0, tiled=True
        ).astype(jnp.float32),
    )
    gain_owned = lax.psum_scatter(
        jnp.stack([grad_gain_one, grad_gain_two]),
        ("group", "replica"),
        scatter_dimension=1,
        tiled=True,
    )
    squares = jnp.stack(
        [
            jnp.sum((source * source).reshape(sequences, -1), axis=1),
            jnp.sum((middle * middle).reshape(sequences, -1), axis=1),
            jnp.sum((output_full * output_full).reshape(sequences, -1), axis=1),
        ],
        axis=1,
    )
    square_totals = lax.psum(squares, "group")
    stream_rms = jnp.sqrt(square_totals / (full_len * model_width))
    layer_out = output_full.astype(jnp.bfloat16).reshape(sequences, block_size, model_width)
    input_grad = input_grad.reshape(sequences, block_size, model_width)
    return (
        layer_out,
        input_grad,
        gain_owned[0],
        grad_query,
        grad_key,
        grad_value,
        grad_out,
        gain_owned[1],
        grad_gate,
        grad_up,
        grad_down,
        stream_rms,
    )


def solution(mesh):
    placed = (
        P("replica", "group", None),
        P("replica", "group"),
        P("replica", None),
        P("group"),
        P("group", None),
        P("group", None),
        P("group", None),
        P("group", None),
        P("group"),
        P("group", None),
        P("group", None),
        P("group", None),
        P("replica", "group", None),
    )
    return jax.shard_map(
        shards,
        mesh=mesh,
        in_specs=placed,
        out_specs=(
            P("replica", "group", None),
            P("replica", "group", None),
            P(("group", "replica")),
            P(("group", "replica"), None),
            P(("group", "replica"), None),
            P(("group", "replica"), None),
            P(("group", "replica"), None),
            P(("group", "replica")),
            P(("group", "replica"), None),
            P(("group", "replica"), None),
            P(("group", "replica"), None),
            P("replica", None),
        ),
        check_vma=False,
    )
```

profile of v0, /device:TPU:0, one launch (start us, length us, event | category | flops | bytes accessed | tf_op | source)
XLA Modules:
  0.0 4407.7 jit_solution(10174914001787924033)
XLA Ops:
  9.4 14.6 all-gather.3
  27.3 50.7 %all-gather.24.cloned.1.call-done = bf16[2560,640]{1,0:T(8,128)(2,1)} async-done(((bf16[640,640]{1,0:T(8,128)(2,1)}), bf16[2560,640]{1,0:T(8,128)(2,1)}) %all-gather.24.cloned.1.call-update) | async-done | bytes 3276816 | tf_op jit(solution)/shard_map/all_gather | solution.py:91
  78.0 4.0 fusion.41
  86.8 57.1 %all-gather.22.cloned.1.call-done = bf16[2560,640]{1,0:T(8,128)(2,1)} async-done(((bf16[640,640]{1,0:T(8,128)(2,1)}), bf16[2560,640]{1,0:T(8,128)(2,1)}) %all-gather.22.cloned.1.call-update) | async-done | bytes 3276816 | tf_op jit(solution)/shard_map/all_gather | solution.py:92
  143.9 3.9 convolution_convert_fusion.8
  153.2 13.6 all-gather.4
  169.8 7.8 all-gather.50.cloned.1.call-done
  179.2 32.1 all-gather.48.cloned.1.call-done
  213.7 224.8 %all-gather.26.cloned.1.call-done = bf16[2560,2560]{1,0:T(8,128)(2,1)} async-done(((bf16[640,2560]{1,0:T(8,128)(2,1)}), bf16[2560,2560]{1,0:T(8,128)(2,1)}) %all-gather.26.cloned.1.call-update) | async-done | bytes 13107216 | tf_op jit(solution)/shard_map/all_gather | solution.py:90
  438.5 8.5 fusion.39
  447.7 14.4 fusion.49
  462.2 13.2 fusion.3
  475.4 13.8 fusion.28
  489.3 175.7 %all-gather.28.cloned.1.call-done = bf16[2560,2560]{1,0:T(8,128)(2,1)} async-done(((bf16[640,2560]{1,0:T(8,128)(2,1)}), bf16[2560,2560]{1,0:T(8,128)(2,1)}) %all-gather.28.cloned.1.call-update) | async-done | bytes 13107216 | tf_op jit(solution)/shard_map/all_gather | solution.py:93
  664.9 7.0 multiply_reduce_fusion.4
  673.9 605.2 %all-gather.30.cloned.1.call-done = bf16[2560,7168]{1,0:T(8,128)(2,1)} async-done(((bf16[640,7168]{1,0:T(8,128)(2,1)}), bf16[2560,7168]{1,0:T(8,128)(2,1)}) %all-gather.30.cloned.1.call-update) | async-done | bytes 36700176 | tf_op jit(solution)/shard_map/all_gather | solution.py:162
  1279.1 24.5 fusion.50
  1303.6 590.1 %all-gather.32.cloned.1.call-done = bf16[2560,7168]{1,0:T(8,128)(2,1)} async-done(((bf16[640,7168]{1,0:T(8,128)(2,1)}), bf16[2560,7168]{1,0:T(8,128)(2,1)}) %all-gather.32.cloned.1.call-update) | async-done | bytes 36700176 | tf_op jit(solution)/shard_map/all_gather | solution.py:163
  1893.7 24.5 fusion.51
  1918.3 590.1 %all-gather.34.cloned.1.call-done = bf16[2560,7168]{1,0:T(8,128)(2,1)} async-done(((bf16[640,7168]{1,0:T(8,128)(2,1)}), bf16[2560,7168]{1,0:T(8,128)(2,1)}) %all-gather.34.cloned.1.call-update) | async-done | bytes 36700176 | tf_op jit(solution)/shard_map/all_gather | solution.py:164
  2508.4 27.7 multiply_convert_fusion
  2536.1 18.5 fusion.52
  2554.6 21.0 multiply_reduce_fusion.1
  2575.6 4.4 fusion.44
  2581.1 8.3 convolution_convert_fusion.5
  2590.0 14.7 fusion.5
  2606.1 22.3 fusion
  2628.4 28.1 fusion.2
  2656.5 12.5 bitcast_multiply_fusion.3
  2671.6 48.2 %reduce-scatter.15.cloned.1.call-done = f32[1,256,640]{1,2,0:T(8,128)} async-done(((f32[1,1024,640]{1,2,0:T(8,128)}), f32[1,256,640]{1,2,0:T(8,128)}) %reduce-scatter.15.cloned.1.call-update) | async-done | bytes 655376 | tf_op jit(solution)/shard_map/reduce_scatter | solution.py:247
  2722.5 9.0 convolution_multiply_fusion
  2737.5 4.3 all-to-all-start.1
  2741.9 6.9 fusion.53
  2751.2 3.1 fusion.18
  2756.1 91.9 %all-gather.40.cloned.1.call-done = bf16[1024,2560]{0,1:T(8,128)(2,1)} async-done(((bf16[256,2560]{0,1:T(8,128)(2,1)}), bf16[1024,2560]{0,1:T(8,128)(2,1)}) %all-gather.40.cloned.1.call-update) | async-done | bytes 5242896 | tf_op jit(solution)/shard_map/all_gather | solution.py:279
  2848.0 8.2 convolution_convert_fusion.3
  2861.0 51.0 %all_to_all.73 = bf16[256,4,640]{2,0,1:T(8,128)(2,1)S(1)} all-to-all(bf16[256,4,640]{2,0,1:T(8,128)(2,1)S(1)} %fusion.27), channel_id=1, replica_groups=mesh['group'=4,'replica'=8] {'group'}, dimensions={1} | all-to-all | bytes 2621440 | tf_op jit(solution)/shard_map/all_to_all | solution.py:270
  2912.0 3.5 convolution_convert_fusion.6
  2915.5 24.7 all-gather.38.cloned.1.call-done
  2940.3 3.4 convolution_convert_fusion.7
  2943.8 94.7 %all-gather.36.cloned.1.call-done = bf16[1024,2560]{0,1:T(8,128)(2,1)} async-done(((bf16[256,2560]{0,1:T(8,128)(2,1)}), bf16[1024,2560]{0,1:T(8,128)(2,1)}) %all-gather.36.cloned.1.call-update) | async-done | bytes 5242896 | tf_op jit(solution)/shard_map/all_gather | solution.py:276
  3038.5 7.8 convolution_convert_fusion.4
  3049.3 76.3 %all_to_all.74 = bf16[256,4,640]{0,2,1:T(8,128)(2,1)S(1)} all-to-all(bf16[256,4,640]{0,2,1:T(8,128)(2,1)} %bitcast.221), channel_id=1, replica_groups=mesh['group'=4,'replica'=8] {'group'}, dimensions={1} | all-to-all | bytes 2621440 | tf_op jit(solution)/shard_map/all_to_all | solution.py:273
  3127.0 191.6 %all-gather.46.cloned.1.call-done = bf16[1024,7168]{1,0:T(8,128)(2,1)} async-done(((bf16[256,7168]{1,0:T(8,128)(2,1)}), bf16[1024,7168]{1,0:T(8,128)(2,1)}) %all-gather.46.cloned.1.call-update) | async-done | bytes 14680080 | tf_op jit(solution)/shard_map/all_gather | solution.py:284
  3318.6 17.5 fusion.9
  3336.1 12.9 copy.109
  3350.5 75.0 %all_to_all.75 = bf16[256,4,640]{2,0,1:T(8,128)(2,1)S(1)} all-to-all(bf16[256,4,640]{2,0,1:T(8,128)(2,1)S(1)} %bitcast.220), channel_id=1, replica_groups=mesh['group'=4,'replica'=8] {'group'}, dimensions={1} | all-to-all | bytes 2621440 | tf_op jit(solution)/shard_map/all_to_all | solution.py:272
  3425.5 173.3 %all-gather.42.cloned.1.call-done = bf16[1024,7168]{1,0:T(8,128)(2,1)} async-done(((bf16[256,7168]{1,0:T(8,128)(2,1)}), bf16[1024,7168]{1,0:T(8,128)(2,1)}) %all-gather.42.cloned.1.call-update) | async-done | bytes 14680080 | tf_op jit(solution)/shard_map/all_gather | solution.py:282
  3598.7 17.4 convolution_convert_fusion.1
  3616.4 234.5 %all-gather.44.cloned.1.call-done = bf16[1024,7168]{1,0:T(8,128)(2,1)} async-done(((bf16[256,7168]{1,0:T(8,128)(2,1)}), bf16[1024,7168]{1,0:T(8,128)(2,1)}) %all-gather.44.cloned.1.call-update) | async-done | bytes 14680080 | tf_op jit(solution)/shard_map/all_gather | solution.py:283
  3850.8 17.4 convolution_convert_fusion
  3869.5 20.0 multiply_reduce_fusion
  3891.5 8.6 psum.7
  3900.7 4.8 fusion.24
  3905.4 81.6 %reduce-scatter.31.cloned.1.call-done = f32[80,2]{1,0:T(8,128)} async-done(((f32[2560,2]{1,0:T(8,128)}), f32[80,2]{1,0:T(8,128)}) %reduce-scatter.31.cloned.1.call-update) | async-done | bytes 656
  3989.1 44.5 %reduce-scatter.25.cloned.1.call-done = bf16[80,2560]{1,0:T(8,128)(2,1)} async-done(((bf16[640,2560]{1,0:T(8,128)(2,1)}), bf16[80,2560]{1,0:T(8,128)(2,1)}) %reduce-scatter.25.cloned.1.call-update) | async-done | bytes 409616 | tf_op jit(solution)/shard_map/reduce_scatter | solution.py:305
  4035.5 36.8 reduce-scatter.23.cloned.1.call-done
  4073.9 36.8 reduce-scatter.21.cloned.1.call-done
  4112.4 49.1 %reduce-scatter.19.cloned.1.call-done = bf16[80,2560]{1,0:T(8,128)(2,1)} async-done(((bf16[640,2560]{1,0:T(8,128)(2,1)}), bf16[80,2560]{1,0:T(8,128)(2,1)}) %reduce-scatter.19.cloned.1.call-update) | async-done | bytes 409616 | tf_op jit(solution)/shard_map/reduce_scatter | solution.py:296
  4163.4 77.1 %reduce-scatter.33.cloned.1.call-done = bf16[80,7168]{1,0:T(8,128)(2,1)} async-done(((bf16[640,7168]{1,0:T(8,128)(2,1)}), bf16[80,7168]{1,0:T(8,128)(2,1)}) %reduce-scatter.33.cloned.1.call-update) | async-done | bytes 1146896
  4244.3 74.9 %reduce-scatter.27.cloned.1.call-done = bf16[80,7168]{1,0:T(8,128)(2,1)} async-done(((bf16[640,7168]{1,0:T(8,128)(2,1)}), bf16[80,7168]{1,0:T(8,128)(2,1)}) %reduce-scatter.27.cloned.1.call-update) | async-done | bytes 1146896 | tf_op jit(solution)/shard_map/reduce_scatter | solution.py:308
  4319.2 2.8 convert_element_type.179
  4322.0 76.2 %reduce-scatter.29.cloned.1.call-done = bf16[80,7168]{1,0:T(8,128)(2,1)} async-done(((bf16[640,7168]{1,0:T(8,128)(2,1)}), bf16[80,7168]{1,0:T(8,128)(2,1)}) %reduce-scatter.29.cloned.1.call-update) | async-done | bytes 1146896 | tf_op jit(solution)/shard_map/reduce_scatter | solution.py:311
  4398.2 2.8 convert_element_type.181
  (196 shorter events, 69.7 us)
Async XLA Ops:
  7.2 70.8 %all-gather.24.cloned.1.call-start = ((), (), s32[]{:S(2)}) async-start(), calls=%async_computation.15 | async-start | bytes 4096000 | tf_op jit(solution)/shard_map/all_gather | solution.py:91
  7.9 18.5 copy-start
  7.9 135.9 %all-gather.22.cloned.1.call-start = ((), (), s32[]{:S(2)}) async-start(), calls=%async_computation.14 | async-start | bytes 4096000 | tf_op jit(solution)/shard_map/all_gather | solution.py:92
  8.7 168.9 %all-gather.50.cloned.1.call-start = ((), (), s32[]{:S(2)}) async-start(), calls=%async_computation.36 | async-start | bytes 1638400 | tf_op jit(solution)/shard_map/all_gather | solution.py:121
  24.0 0.6 copy-start.29
  24.7 413.8 %copy-start.27 = (f32[2560]{0:T(1024)}, f32[2560]{0:T(1024)S(1)}, u32[]{:S(2)}) copy-start(f32[2560]{0:T(1024)S(1)} %reshape.535) | copy-start | bytes 30724
  25.8 421.4 %copy-start.22 = (f32[256,80]{0,1:T(8,128)}, f32[256,80]{0,1:T(8,128)S(1)}, u32[]{:S(2)}) copy-start(f32[256,80]{0,1:T(8,128)S(1)} %get-tuple-element.147) | copy-start | bytes 245764
  25.8 421.4 %copy-start.24 = (f32[256,80]{0,1:T(8,128)}, f32[256,80]{0,1:T(8,128)S(1)}, u32[]{:S(2)}) copy-start(f32[256,80]{0,1:T(8,128)S(1)} %get-tuple-element.148) | copy-start | bytes 245764
  27.3 411.2 %copy-start.31 = (f32[256]{0:T(256)}, f32[256]{0:T(256)S(1)}, u32[]{:S(2)}) copy-start(f32[256]{0:T(256)S(1)} %get-tuple-element.150) | copy-start | bytes 3076
  86.8 124.5 %all-gather.48.cloned.1.call-start = ((), (), s32[]{:S(2)}) async-start(), calls=%async_computation.35 | async-start | bytes 1638400 | tf_op jit(solution)/shard_map/all_gather | solution.py:122
  147.8 290.7 %all-gather.26.cloned.1.call-start = ((), (), s32[]{:S(2)}) async-start(), calls=%async_computation.16 | async-start | bytes 16384000 | tf_op jit(solution)/shard_map/all_gather | solution.py:90
  148.4 516.5 %all-gather.28.cloned.1.call-start = ((), (), s32[]{:S(2)}) async-start(), calls=%async_computation.17 | async-start | bytes 16384000 | tf_op jit(solution)/shard_map/all_gather | solution.py:93
  149.0 1130.1 %all-gather.30.cloned.1.call-start = ((), (), s32[]{:S(2)}) async-start(), calls=%async_computation.18 | async-start | bytes 45875200 | tf_op jit(solution)/shard_map/all_gather | solution.py:162
  149.7 1744.0 %all-gather.32.cloned.1.call-start = ((), (), s32[]{:S(2)}) async-start(), calls=%async_computation.19 | async-start | bytes 45875200 | tf_op jit(solution)/shard_map/all_gather | solution.py:163
  150.5 0.8 copy-start.35
  150.5 2.7 copy-start.34
  150.5 2357.9 %all-gather.34.cloned.1.call-start = ((), (), s32[]{:S(2)}) async-start(), calls=%async_computation.20 | async-start | bytes 45875200 | tf_op jit(solution)/shard_map/all_gather | solution.py:164
  151.2 2518.5 %reduce-scatter.17.cloned.1.call-start = ((), (), s32[]{:S(2)}) async-start(), calls=%async_computation.22 | async-start | bytes 3276800 | tf_op jit(solution)/shard_map/reduce_scatter | solution.py:248
  179.2 268.6 %copy-start.4 = (bf16[1024,640]{0,1:T(8,128)(2,1)}, bf16[1024,640]{0,1:T(8,128)(2,1)S(1)}, u32[]{:S(2)}) copy-start(bf16[1024,640]{0,1:T(8,128)(2,1)S(1)} %copy.84) | copy-start | bytes 3932164
  447.7 14.4 copy-start.2
  462.1 13.3 copy-start.8
  489.2 182.7 %copy-start.26 = (bf16[8,80,4,256]{3,1,2,0:T(8,128)(2,1)}, bf16[8,80,4,256]{3,1,2,0:T(8,128)(2,1)S(1)}, u32[]{:S(2)}) copy-start(bf16[8,80,4,256]{3,1,2,0:T(8,128)(2,1)S(1)} %fusion.28) | copy-start | bytes 3932164
  672.0 1.6 copy-start.6
  673.9 1219.8 %copy-start.12 = (bf16[256,2560]{1,0:T(8,128)(2,1)}, bf16[256,2560]{1,0:T(8,128)(2,1)S(1)}, u32[]{:S(2)}) copy-start(bf16[256,2560]{1,0:T(8,128)(2,1)S(1)} %multiply_convert_fusion.3) | copy-start | bytes 3932164
  1303.6 1204.8 %copy-start.10 = (bf16[1,256,2560]{2,1,0:T(8,128)(2,1)S(1)}, bf16[1,256,2560]{2,1,0:T(8,128)(2,1)}, u32[]{:S(2)}) copy-start(bf16[1,256,2560]{2,1,0:T(8,128)(2,1)} %param.25) | copy-start | bytes 3932164
  2536.1 18.5 copy-start.7
  2580.0 1.1 copy-start.14
  2604.7 1.3 copy-start.9
  2604.8 115.0 %reduce-scatter.15.cloned.1.call-start = ((), (), s32[]{:S(2)}) async-start(), calls=%async_computation.21 | async-start | bytes 3276800 | tf_op jit(solution)/shard_map/reduce_scatter | solution.py:247
  2628.4 28.1 copy-start.3
  2669.0 50.8 %copy-start.25 = (f32[256,80]{0,1:T(8,128)S(1)}, f32[256,80]{0,1:T(8,128)}, u32[]{:S(2)}) copy-start(f32[256,80]{0,1:T(8,128)} %copy-done.24) | copy-start | bytes 245764
  2669.0 178.9 %all-gather.40.cloned.1.call-start = ((), (), s32[]{:S(2)}) async-start(), calls=%async_computation.28 | async-start | bytes 6553600 | tf_op jit(solution)/shard_map/all_gather | solution.py:279
  2669.6 51.5 %copy-start.23 = (f32[256,80]{0,1:T(8,128)S(1)}, f32[256,80]{0,1:T(8,128)}, u32[]{:S(2)}) copy-start(f32[256,80]{0,1:T(8,128)} %copy-done.22) | copy-start | bytes 245764
  2669.6 242.4 %all-gather.52.cloned.1.call-start = ((), (), s32[]{:S(2)}) async-start(), calls=%async_computation.37 | async-start | bytes 1638400 | tf_op jit(solution)/shard_map/all_gather | solution.py:278
  2671.6 268.7 %all-gather.38.cloned.1.call-start = ((), (), s32[]{:S(2)}) async-start(), calls=%async_computation.25 | async-start | bytes 1638400 | tf_op jit(solution)/shard_map/all_gather | solution.py:277
  2719.8 1.4 copy-start.21
  2721.0 1.5 copy-start.5
  2722.0 316.5 %all-gather.36.cloned.1.call-start = ((), (), s32[]{:S(2)}) async-start(), calls=%async_computation.23 | async-start | bytes 6553600 | tf_op jit(solution)/shard_map/all_gather | solution.py:276
  2733.8 584.8 %all-gather.46.cloned.1.call-start = ((), (), s32[]{:S(2)}) async-start(), calls=%async_computation.34 | async-start | bytes 18350080 | tf_op jit(solution)/shard_map/all_gather | solution.py:284
  2734.4 864.3 %all-gather.42.cloned.1.call-start = ((), (), s32[]{:S(2)}) async-start(), calls=%async_computation.30 | async-start | bytes 18350080 | tf_op jit(solution)/shard_map/all_gather | solution.py:282
  2735.0 1.3 copy-start.15
  2735.0 1115.8 %all-gather.44.cloned.1.call-start = ((), (), s32[]{:S(2)}) async-start(), calls=%async_computation.32 | async-start | bytes 18350080 | tf_op jit(solution)/shard_map/all_gather | solution.py:283
  2736.3 5.6 copy-start.16
  2737.5 110.5 %all-to-all-start.1 = ((bf16[256,4,640]{2,0,1:T(8,128)(2,1)}), bf16[256,4,640]{2,0,1:T(8,128)(2,1)}, u32[]{:S(2)}, u32[]{:S(2)}) async-start(bf16[256,4,640]{2,0,1:T(8,128)(2,1)} %bitcast.218), calls=%async_computation.6 | async-start | bytes 2621440 | tf_op jit(solution)/shard_map/all_to_all | solution.py:271
  2741.8 7.0 copy-start.20
  2741.8 1245.2 %reduce-scatter.31.cloned.1.call-start = ((), (), s32[]{:S(2)}) async-start(), calls=%async_computation.38 | async-start | bytes 1351680
  2741.9 6.9 copy-start.17
  2748.8 1.3 copy-start.1
  2748.8 2.3 copy-start.18
  2748.8 2.3 copy-start.19
  2748.8 2.3 copy-start.28
  2748.9 2.3 copy-start.32
  2755.8 1277.8 %reduce-scatter.25.cloned.1.call-start = ((), (), s32[]{:S(2)}) async-start(), calls=%async_computation.29 | async-start | bytes 3686400 | tf_op jit(solution)/shard_map/reduce_scatter | solution.py:305
  2856.2 0.7 copy-start.30
  2856.2 1216.2 %reduce-scatter.23.cloned.1.call-start = ((), (), s32[]{:S(2)}) async-start(), calls=%async_computation.27 | async-start | bytes 921600 | tf_op jit(solution)/shard_map/reduce_scatter | solution.py:302
  2915.5 1195.3 %reduce-scatter.21.cloned.1.call-start = ((), (), s32[]{:S(2)}) async-start(), calls=%async_computation.26 | async-start | bytes 921600 | tf_op jit(solution)/shard_map/reduce_scatter | solution.py:299
  2943.7 1217.8 %reduce-scatter.19.cloned.1.call-start = ((), (), s32[]{:S(2)}) async-start(), calls=%async_computation.24 | async-start | bytes 3686400 | tf_op jit(solution)/shard_map/reduce_scatter | solution.py:296
  3046.4 1.6 copy-start.11
  3046.4 1194.1 %reduce-scatter.33.cloned.1.call-start = ((), (), s32[]{:S(2)}) async-start(), calls=%async_computation.39 | async-start | bytes 10321920
  3349.0 1.3 copy-start.13
  3349.1 970.1 %reduce-scatter.27.cloned.1.call-start = ((), (), s32[]{:S(2)}) async-start(), calls=%async_computation.31 | async-start | bytes 10321920 | tf_op jit(solution)/shard_map/reduce_scatter | solution.py:308
  3616.1 782.0 %reduce-scatter.29.cloned.1.call-start = ((), (), s32[]{:S(2)}) async-start(), calls=%async_computation.33 | async-start | bytes 10321920 | tf_op jit(solution)/shard_map/reduce_scatter | solution.py:311
  3869.5 31.1 copy-start.33
Sparse Core Ops, SparseCore 0:
  9.6 68.3 all-gather.23
  79.5 64.2 all-gather.21
  146.0 31.4 all-gather.49
  179.5 31.6 all-gather.47
  212.7 225.7 all-gather.25
  439.9 224.9 all-gather.27
  666.5 612.5 all-gather.29
  1280.6 613.0 all-gather.31
  1895.3 613.0 all-gather.33
  2604.9 50.8 reduce-scatter.16
  2669.2 50.5 reduce-scatter.14
  2721.2 126.6 all-gather.39
  2850.1 56.3 all-gather.51
  2908.5 31.7 all-gather.37
  2942.2 96.2 all-gather.35
  3039.9 278.6 all-gather.45
  3320.1 278.6 all-gather.41
  3600.2 250.6 all-gather.43
  3853.6 133.3 reduce-scatter.30
  3990.7 42.8 reduce-scatter.24
  4037.8 34.4 reduce-scatter.22
  4076.3 34.4 reduce-scatter.20
  4114.6 46.8 reduce-scatter.18
  4165.4 75.0 reduce-scatter.32
  4244.1 75.0 reduce-scatter.26
  4323.1 75.0 reduce-scatter.28
where the time goes:
time: 4410 us
  waiting for transfers between devices  3680 us (83%)
  matrix products  341 us (8%)
  blocking collectives  239 us (5%)
  other arithmetic  83.8 us (2%)
  local copies, waits for them, and re-layouts  45.3 us (1%)
    all_gather x1, waiting for transfers between devices, shards(): gate_piece = lax.all_gather(w_gate, 'group', axis=0, tiled=True)  605 us
    all_gather x1, waiting for transfers between devices, shards(): down_piece = lax.all_gather(w_down, 'group', axis=0, tiled=True)  590 us
    all_gather x1, waiting for transfers between devices, shards(): up_piece = lax.all_gather(w_up, 'group', axis=0, tiled=True)  590 us
    all_gather x1, waiting for transfers between devices, shards(): lax.all_gather(grad_lift_low, 'group', axis=0, tiled=True)  234 us
    all_gather x1, waiting for transfers between devices, shards(): query_piece = lax.all_gather(w_query, 'group', axis=0, tiled=True)  225 us
    all_gather x1, waiting for transfers between devices, shards(): lax.all_gather(hidden, 'group', axis=0, tiled=True)  192 us
    all_gather x1, waiting for transfers between devices, shards(): out_piece = lax.all_gather(w_out, 'group', axis=0, tiled=True)  176 us
    all_gather x1, waiting for transfers between devices, shards(): lax.all_gather(grad_gate_low, 'group', axis=0, tiled=True)  173 us
  transfers between devices with their start and end apart: 27, of which 24 were waited for; matrix products, arithmetic and copies ran while one was open for 8% of the time, Pallas kernels for 0%

commit v1 on v0

--- a/solution.py
+++ b/solution.py
@@ -160,8 +160,11 @@
     unit_two = middle * inverse_two
     gain_piece = lax.all_gather(gain_mlp, "group", axis=0, tiled=True)
     gate_piece = lax.all_gather(w_gate, "group", axis=0, tiled=True)
-    up_piece = lax.all_gather(w_up, "group", axis=0, tiled=True)
-    down_piece = lax.all_gather(w_down, "group", axis=0, tiled=True)
+    up_piece, down_piece = jnp.split(
+        lax.all_gather(jnp.concatenate([w_up, w_down], axis=1), "group", axis=0, tiled=True),
+        [w_up.shape[1]],
+        axis=1,
+    )
     scaled = unit_two * gain_piece.astype(jnp.float32)
     scaled = scaled.astype(jnp.bfloat16)
     gated = jnp.dot(scaled, gate_piece, preferred_element_type=jnp.float32)

time: 4410 us -> 4970 us (1.13)
  waiting for transfers between devices: 3680 us -> 4210 us
    all_gather x1, waiting for transfers between devices: 590 us -> 1190 us  [shards(): lax.all_gather(jnp.concatenate([w_up, w_down], axis=1), 'group', axis=0,...]
  transfers between devices with their start and end apart: 27 -> 27, of which waited for: 24 -> 23; matrix products, arithmetic and copies ran while one was open for 8% -> 9% of each run, Pallas kernels for 0% -> 0%
where the time goes in v1:
time: 4970 us; the launch traced here: 4960 us
  waiting for transfers between devices  4210 us (85%)
  matrix products  341 us (7%)
  blocking collectives  239 us (5%)
  other arithmetic  99.9 us (2%)
    all_gather x1, waiting for transfers between devices, shards(): lax.all_gather(jnp.concatenate([w_up, w_down], axis=1), 'group', axis=0,...  1190 us
    all_gather x1, waiting for transfers between devices, shards(): gate_piece = lax.all_gather(w_gate, 'group', axis=0, tiled=True)  605 us
    all_gather x1, waiting for transfers between devices, shards(): up_piece = lax.all_gather(w_up, 'group', axis=0, tiled=True)  547 us
    all_gather x1, waiting for transfers between devices, shards(): lax.all_gather(grad_lift_low, 'group', axis=0, tiled=True)  234 us
    all_gather x1, waiting for transfers between devices, shards(): query_piece = lax.all_gather(w_query, 'group', axis=0, tiled=True)  225 us
    all_gather x1, waiting for transfers between devices, shards(): lax.all_gather(hidden, 'group', axis=0, tiled=True)  192 us
    all_gather x1, waiting for transfers between devices, shards(): out_piece = lax.all_gather(w_out, 'group', axis=0, tiled=True)  176 us
    all_gather x1, waiting for transfers between devices, shards(): lax.all_gather(grad_gate_low, 'group', axis=0, tiled=True)  173 us
  transfers between devices with their start and end apart: 27, of which 23 were waited for; matrix products, arithmetic and copies ran while one was open for 9% of the time, Pallas kernels for 0%

profile of v1, /device:TPU:0, one launch (start us, length us, event | category | flops | bytes accessed | tf_op | source)
XLA Modules:
  0.0 4961.3 jit_solution(207737675268706585)
XLA Ops:
  9.4 14.6 all-gather.3
  27.3 50.7 %all-gather.24.cloned.1.call-done = bf16[2560,640]{1,0:T(8,128)(2,1)} async-done(((bf16[640,640]{1,0:T(8,128)(2,1)}), bf16[2560,640]{1,0:T(8,128)(2,1)}) %all-gather.24.cloned.1.call-update) | async-done | bytes 3276816 | tf_op jit(solution)/shard_map/all_gather | solution.py:91
  78.0 4.0 fusion.52
  86.8 57.1 %all-gather.22.cloned.1.call-done = bf16[2560,640]{1,0:T(8,128)(2,1)} async-done(((bf16[640,640]{1,0:T(8,128)(2,1)}), bf16[2560,640]{1,0:T(8,128)(2,1)}) %all-gather.22.cloned.1.call-update) | async-done | bytes 3276816 | tf_op jit(solution)/shard_map/all_gather | solution.py:92
  143.9 3.9 convolution_convert_fusion.8
  149.8 16.1 pad_maximum_fusion
  168.6 13.1 all-gather.4
  186.5 24.8 all-gather.48.cloned.1.call-done
  213.7 224.8 %all-gather.26.cloned.1.call-done = bf16[2560,2560]{1,0:T(8,128)(2,1)} async-done(((bf16[640,2560]{1,0:T(8,128)(2,1)}), bf16[2560,2560]{1,0:T(8,128)(2,1)}) %all-gather.26.cloned.1.call-update) | async-done | bytes 13107216 | tf_op jit(solution)/shard_map/all_gather | solution.py:90
  438.5 8.5 fusion.50
  447.7 14.4 fusion.60
  462.2 13.2 fusion.9
  475.4 13.8 fusion.40
  489.3 175.6 %all-gather.28.cloned.1.call-done = bf16[2560,2560]{1,0:T(8,128)(2,1)} async-done(((bf16[640,2560]{1,0:T(8,128)(2,1)}), bf16[2560,2560]{1,0:T(8,128)(2,1)}) %all-gather.28.cloned.1.call-update) | async-done | bytes 13107216 | tf_op jit(solution)/shard_map/all_gather | solution.py:93
  664.9 7.1 multiply_reduce_fusion.4
  673.9 605.1 %all-gather.30.cloned.1.call-done = bf16[2560,7168]{1,0:T(8,128)(2,1)} async-done(((bf16[640,7168]{1,0:T(8,128)(2,1)}), bf16[2560,7168]{1,0:T(8,128)(2,1)}) %all-gather.30.cloned.1.call-update) | async-done | bytes 36700176 | tf_op jit(solution)/shard_map/all_gather | solution.py:162
  1279.0 26.7 fusion.63
  1305.7 1188.6 %all-gather.32.cloned.1.call-done = bf16[2560,14336]{1,0:T(8,128)(2,1)} async-done(((bf16[640,14336]{1,0:T(8,128)(2,1)}), bf16[2560,14336]{1,0:T(8,128)(2,1)}) %all-gather.32.cloned.1.call-update) | async-done | bytes 73400336 | tf_op jit(solution)/shard_map/all_gather | solution.py:164
  2494.3 23.2 fusion
  2517.5 25.2 multiply_convert_fusion
  2542.7 19.2 fusion.64
  2561.9 546.6 %all-gather.34.cloned.1.call-done = bf16[2560,7168]{1,0:T(8,128)(2,1)} async-done(((bf16[640,7168]{1,0:T(8,128)(2,1)}), bf16[2560,7168]{1,0:T(8,128)(2,1)}) %all-gather.34.cloned.1.call-update) | async-done | bytes 36700176 | tf_op jit(solution)/shard_map/all_gather | solution.py:189
  3108.6 20.6 multiply_reduce_fusion.1
  3129.1 4.5 fusion.55
  3134.7 8.3 convolution_convert_fusion.5
  3143.6 14.9 fusion.11
  3159.8 22.2 fusion.2
  3182.1 28.1 fusion.4
  3210.2 12.6 bitcast_multiply_fusion.3
  3225.4 48.2 reduce-scatter.15.cloned.1.call-done
  3276.2 9.1 convolution_multiply_fusion
  3291.2 4.3 all-to-all-start.1
  3295.6 7.4 fusion.65
  3305.4 3.1 fusion.30
  3310.1 91.6 %all-gather.40.cloned.1.call-done = bf16[1024,2560]{0,1:T(8,128)(2,1)} async-done(((bf16[256,2560]{0,1:T(8,128)(2,1)}), bf16[1024,2560]{0,1:T(8,128)(2,1)}) %all-gather.40.cloned.1.call-update) | async-done | bytes 5242896 | tf_op jit(solution)/shard_map/all_gather | solution.py:282
  3401.7 8.2 convolution_convert_fusion.3
  3414.7 50.8 %all_to_all.73 = bf16[256,4,640]{2,0,1:T(8,128)(2,1)S(1)} all-to-all(bf16[256,4,640]{2,0,1:T(8,128)(2,1)S(1)} %fusion.39), channel_id=1, replica_groups=mesh['group'=4,'replica'=8] {'group'}, dimensions={1} | all-to-all | bytes 2621440 | tf_op jit(solution)/shard_map/all_to_all | solution.py:273
  3465.5 3.5 convolution_convert_fusion.6
  3469.2 24.5 all-gather.38.cloned.1.call-done
  3493.7 3.4 convolution_convert_fusion.7
  3497.3 94.7 %all-gather.36.cloned.1.call-done = bf16[1024,2560]{0,1:T(8,128)(2,1)} async-done(((bf16[256,2560]{0,1:T(8,128)(2,1)}), bf16[1024,2560]{0,1:T(8,128)(2,1)}) %all-gather.36.cloned.1.call-update) | async-done | bytes 5242896 | tf_op jit(solution)/shard_map/all_gather | solution.py:279
  3592.0 7.8 convolution_convert_fusion.4
  3602.8 76.3 %all_to_all.74 = bf16[256,4,640]{0,2,1:T(8,128)(2,1)S(1)} all-to-all(bf16[256,4,640]{0,2,1:T(8,128)(2,1)} %bitcast.220), channel_id=1, replica_groups=mesh['group'=4,'replica'=8] {'group'}, dimensions={1} | all-to-all | bytes 2621440 | tf_op jit(solution)/shard_map/all_to_all | solution.py:276
  3680.5 191.6 %all-gather.46.cloned.1.call-done = bf16[1024,7168]{1,0:T(8,128)(2,1)} async-done(((bf16[256,7168]{1,0:T(8,128)(2,1)}), bf16[1024,7168]{1,0:T(8,128)(2,1)}) %all-gather.46.cloned.1.call-update) | async-done | bytes 14680080 | tf_op jit(solution)/shard_map/all_gather | solution.py:287
  3872.1 17.5 fusion.15
  3889.6 12.9 copy.114
  3903.9 75.0 %all_to_all.75 = bf16[256,4,640]{2,0,1:T(8,128)(2,1)S(1)} all-to-all(bf16[256,4,640]{2,0,1:T(8,128)(2,1)S(1)} %bitcast.219), channel_id=1, replica_groups=mesh['group'=4,'replica'=8] {'group'}, dimensions={1} | all-to-all | bytes 2621440 | tf_op jit(solution)/shard_map/all_to_all | solution.py:275
  3978.9 173.3 %all-gather.42.cloned.1.call-done = bf16[1024,7168]{1,0:T(8,128)(2,1)} async-done(((bf16[256,7168]{1,0:T(8,128)(2,1)}), bf16[1024,7168]{1,0:T(8,128)(2,1)}) %all-gather.42.cloned.1.call-update) | async-done | bytes 14680080 | tf_op jit(solution)/shard_map/all_gather | solution.py:285
  4152.2 17.4 convolution_convert_fusion.1
  4169.9 234.4 %all-gather.44.cloned.1.call-done = bf16[1024,7168]{1,0:T(8,128)(2,1)} async-done(((bf16[256,7168]{1,0:T(8,128)(2,1)}), bf16[1024,7168]{1,0:T(8,128)(2,1)}) %all-gather.44.cloned.1.call-update) | async-done | bytes 14680080 | tf_op jit(solution)/shard_map/all_gather | solution.py:286
  4404.3 17.4 convolution_convert_fusion
  4423.0 20.2 multiply_reduce_fusion
  4445.2 8.6 psum.7
  4454.4 4.8 fusion.36
  4459.1 81.5 %reduce-scatter.31.cloned.1.call-done = f32[80,2]{1,0:T(8,128)} async-done(((f32[2560,2]{1,0:T(8,128)}), f32[80,2]{1,0:T(8,128)}) %reduce-scatter.31.cloned.1.call-update) | async-done | bytes 656
  4542.7 44.4 reduce-scatter.25.cloned.1.call-done
  4589.1 36.8 reduce-scatter.23.cloned.1.call-done
  4627.5 36.8 reduce-scatter.21.cloned.1.call-done
  4665.9 49.1 reduce-scatter.19.cloned.1.call-done
  4717.0 77.1 %reduce-scatter.33.cloned.1.call-done = bf16[80,7168]{1,0:T(8,128)(2,1)} async-done(((bf16[640,7168]{1,0:T(8,128)(2,1)}), bf16[80,7168]{1,0:T(8,128)(2,1)}) %reduce-scatter.33.cloned.1.call-update) | async-done | bytes 1146896
  4797.8 74.9 %reduce-scatter.27.cloned.1.call-done = bf16[80,7168]{1,0:T(8,128)(2,1)} async-done(((bf16[640,7168]{1,0:T(8,128)(2,1)}), bf16[80,7168]{1,0:T(8,128)(2,1)}) %reduce-scatter.27.cloned.1.call-update) | async-done | bytes 1146896 | tf_op jit(solution)/shard_map/reduce_scatter | solution.py:311
  4872.7 2.8 convert_element_type.179
  4875.5 76.2 %reduce-scatter.29.cloned.1.call-done = bf16[80,7168]{1,0:T(8,128)(2,1)} async-done(((bf16[640,7168]{1,0:T(8,128)(2,1)}), bf16[80,7168]{1,0:T(8,128)(2,1)}) %reduce-scatter.29.cloned.1.call-update) | async-done | bytes 1146896 | tf_op jit(solution)/shard_map/reduce_scatter | solution.py:314
  4951.7 2.8 convert_element_type.181
  (197 shorter events, 69.1 us)
Async XLA Ops:
  7.2 70.8 %all-gather.24.cloned.1.call-start = ((), (), s32[]{:S(2)}) async-start(), calls=%async_computation.15 | async-start | bytes 4096000 | tf_op jit(solution)/shard_map/all_gather | solution.py:91
  7.9 18.5 copy-start
  7.9 136.0 %all-gather.22.cloned.1.call-start = ((), (), s32[]{:S(2)}) async-start(), calls=%async_computation.14 | async-start | bytes 4096000 | tf_op jit(solution)/shard_map/all_gather | solution.py:92
  8.7 176.1 %all-gather.50.cloned.1.call-start = ((), (), s32[]{:S(2)}) async-start(), calls=%async_computation.36 | async-start | bytes 1638400 | tf_op jit(solution)/shard_map/all_gather | solution.py:121
  24.0 0.6 copy-start.29
  24.7 413.8 %copy-start.27 = (f32[2560]{0:T(1024)}, f32[2560]{0:T(1024)S(1)}, u32[]{:S(2)}) copy-start(f32[2560]{0:T(1024)S(1)} %reshape.535) | copy-start | bytes 30724
  25.8 421.4 %copy-start.22 = (f32[256,80]{0,1:T(8,128)}, f32[256,80]{0,1:T(8,128)S(1)}, u32[]{:S(2)}) copy-start(f32[256,80]{0,1:T(8,128)S(1)} %get-tuple-element.147) | copy-start | bytes 245764
  25.8 421.4 %copy-start.24 = (f32[256,80]{0,1:T(8,128)}, f32[256,80]{0,1:T(8,128)S(1)}, u32[]{:S(2)}) copy-start(f32[256,80]{0,1:T(8,128)S(1)} %get-tuple-element.148) | copy-start | bytes 245764
  27.3 411.1 %copy-start.31 = (f32[256]{0:T(256)}, f32[256]{0:T(256)S(1)}, u32[]{:S(2)}) copy-start(f32[256]{0:T(256)S(1)} %get-tuple-element.150) | copy-start | bytes 3076
  86.8 124.5 %all-gather.48.cloned.1.call-start = ((), (), s32[]{:S(2)}) async-start(), calls=%async_computation.35 | async-start | bytes 1638400 | tf_op jit(solution)/shard_map/all_gather | solution.py:122
  147.8 290.7 %all-gather.26.cloned.1.call-start = ((), (), s32[]{:S(2)}) async-start(), calls=%async_computation.16 | async-start | bytes 16384000 | tf_op jit(solution)/shard_map/all_gather | solution.py:90
  148.4 516.5 %all-gather.28.cloned.1.call-start = ((), (), s32[]{:S(2)}) async-start(), calls=%async_computation.17 | async-start | bytes 16384000 | tf_op jit(solution)/shard_map/all_gather | solution.py:93
  149.0 1130.1 %all-gather.30.cloned.1.call-start = ((), (), s32[]{:S(2)}) async-start(), calls=%async_computation.18 | async-start | bytes 45875200 | tf_op jit(solution)/shard_map/all_gather | solution.py:162
  149.7 2344.6 %all-gather.32.cloned.1.call-start = ((), (), s32[]{:S(2)}) async-start(), calls=%async_computation.19 | async-start | bytes 91750400 | tf_op jit(solution)/shard_map/all_gather | solution.py:164
  165.9 0.8 copy-start.35
  165.9 2.7 copy-start.34
  165.9 2942.7 %all-gather.34.cloned.1.call-start = ((), (), s32[]{:S(2)}) async-start(), calls=%async_computation.20 | async-start | bytes 45875200 | tf_op jit(solution)/shard_map/all_gather | solution.py:189
  166.6 3056.8 %reduce-scatter.17.cloned.1.call-start = ((), (), s32[]{:S(2)}) async-start(), calls=%async_computation.22 | async-start | bytes 3276800 | tf_op jit(solution)/shard_map/reduce_scatter | solution.py:251
  186.5 261.3 %copy-start.4 = (bf16[1024,640]{0,1:T(8,128)(2,1)}, bf16[1024,640]{0,1:T(8,128)(2,1)S(1)}, u32[]{:S(2)}) copy-start(bf16[1024,640]{0,1:T(8,128)(2,1)S(1)} %copy.87) | copy-start | bytes 3932164
  447.7 14.4 copy-start.2
  462.2 13.3 copy-start.8
  489.2 182.7 %copy-start.26 = (bf16[8,80,4,256]{3,1,2,0:T(8,128)(2,1)}, bf16[8,80,4,256]{3,1,2,0:T(8,128)(2,1)S(1)}, u32[]{:S(2)}) copy-start(bf16[8,80,4,256]{3,1,2,0:T(8,128)(2,1)S(1)} %fusion.40) | copy-start | bytes 3932164
  672.0 1.6 copy-start.6
  673.9 1820.4 %copy-start.12 = (bf16[256,2560]{1,0:T(8,128)(2,1)}, bf16[256,2560]{1,0:T(8,128)(2,1)S(1)}, u32[]{:S(2)}) copy-start(bf16[256,2560]{1,0:T(8,128)(2,1)S(1)} %multiply_convert_fusion.3) | copy-start | bytes 3932164
  1305.7 1211.8 %copy-start.10 = (bf16[1,256,2560]{2,1,0:T(8,128)(2,1)S(1)}, bf16[1,256,2560]{2,1,0:T(8,128)(2,1)}, u32[]{:S(2)}) copy-start(bf16[1,256,2560]{2,1,0:T(8,128)(2,1)} %param.25) | copy-start | bytes 3932164
  2542.7 565.8 %copy-start.7 = (f32[256,2560]{1,0:T(8,128)S(1)}, f32[256,2560]{1,0:T(8,128)}, u32[]{:S(2)}) copy-start(f32[256,2560]{1,0:T(8,128)} %copy-done.6) | copy-start | bytes 7864324
  3133.6 1.1 copy-start.14
  3158.5 1.3 copy-start.9
  3158.5 115.0 %reduce-scatter.15.cloned.1.call-start = ((), (), s32[]{:S(2)}) async-start(), calls=%async_computation.21 | async-start | bytes 3276800 | tf_op jit(solution)/shard_map/reduce_scatter | solution.py:250
  3182.1 28.1 copy-start.3
  3222.8 50.8 %copy-start.25 = (f32[256,80]{0,1:T(8,128)S(1)}, f32[256,80]{0,1:T(8,128)}, u32[]{:S(2)}) copy-start(f32[256,80]{0,1:T(8,128)} %copy-done.24) | copy-start | bytes 245764
  3222.8 178.9 %all-gather.40.cloned.1.call-start = ((), (), s32[]{:S(2)}) async-start(), calls=%async_computation.28 | async-start | bytes 6553600 | tf_op jit(solution)/shard_map/all_gather | solution.py:282
  3223.4 51.5 %copy-start.23 = (f32[256,80]{0,1:T(8,128)S(1)}, f32[256,80]{0,1:T(8,128)}, u32[]{:S(2)}) copy-start(f32[256,80]{0,1:T(8,128)} %copy-done.22) | copy-start | bytes 245764
  3223.4 242.1 %all-gather.52.cloned.1.call-start = ((), (), s32[]{:S(2)}) async-start(), calls=%async_computation.37 | async-start | bytes 1638400 | tf_op jit(solution)/shard_map/all_gather | solution.py:281
  3225.3 268.4 %all-gather.38.cloned.1.call-start = ((), (), s32[]{:S(2)}) async-start(), calls=%async_computation.25 | async-start | bytes 1638400 | tf_op jit(solution)/shard_map/all_gather | solution.py:280
  3273.5 1.4 copy-start.21
  3274.8 1.5 copy-start.5
  3275.7 316.2 %all-gather.36.cloned.1.call-start = ((), (), s32[]{:S(2)}) async-start(), calls=%async_computation.23 | async-start | bytes 6553600 | tf_op jit(solution)/shard_map/all_gather | solution.py:279
  3287.6 584.6 %all-gather.46.cloned.1.call-start = ((), (), s32[]{:S(2)}) async-start(), calls=%async_computation.34 | async-start | bytes 18350080 | tf_op jit(solution)/shard_map/all_gather | solution.py:287
  3288.1 864.1 %all-gather.42.cloned.1.call-start = ((), (), s32[]{:S(2)}) async-start(), calls=%async_computation.30 | async-start | bytes 18350080 | tf_op jit(solution)/shard_map/all_gather | solution.py:285
  3288.7 1.3 copy-start.15
  3288.7 1115.6 %all-gather.44.cloned.1.call-start = ((), (), s32[]{:S(2)}) async-start(), calls=%async_computation.32 | async-start | bytes 18350080 | tf_op jit(solution)/shard_map/all_gather | solution.py:286
  3290.1 5.6 copy-start.16
  3291.2 110.5 %all-to-all-start.1 = ((bf16[256,4,640]{2,0,1:T(8,128)(2,1)}), bf16[256,4,640]{2,0,1:T(8,128)(2,1)}, u32[]{:S(2)}, u32[]{:S(2)}) async-start(bf16[256,4,640]{2,0,1:T(8,128)(2,1)} %bitcast.217), calls=%async_computation.6 | async-start | bytes 2621440 | tf_op jit(solution)/shard_map/all_to_all | solution.py:274
  3295.6 7.5 copy-start.20
  3295.6 1245.0 %reduce-scatter.31.cloned.1.call-start = ((), (), s32[]{:S(2)}) async-start(), calls=%async_computation.38 | async-start | bytes 1351680
  3295.6 7.4 copy-start.17
  3303.0 1.3 copy-start.1
  3303.0 2.3 copy-start.18
  3303.0 2.3 copy-start.19
  3303.1 2.3 copy-start.28
  3303.1 2.3 copy-start.32
  3310.0 1277.1 %reduce-scatter.25.cloned.1.call-start = ((), (), s32[]{:S(2)}) async-start(), calls=%async_computation.29 | async-start | bytes 3686400 | tf_op jit(solution)/shard_map/reduce_scatter | solution.py:308
  3409.9 0.7 copy-start.30
  3409.9 1216.0 %reduce-scatter.23.cloned.1.call-start = ((), (), s32[]{:S(2)}) async-start(), calls=%async_computation.27 | async-start | bytes 921600 | tf_op jit(solution)/shard_map/reduce_scatter | solution.py:305
  3469.0 1195.4 %reduce-scatter.21.cloned.1.call-start = ((), (), s32[]{:S(2)}) async-start(), calls=%async_computation.26 | async-start | bytes 921600 | tf_op jit(solution)/shard_map/reduce_scatter | solution.py:302
  3497.2 1217.8 %reduce-scatter.19.cloned.1.call-start = ((), (), s32[]{:S(2)}) async-start(), calls=%async_computation.24 | async-start | bytes 3686400 | tf_op jit(solution)/shard_map/reduce_scatter | solution.py:299
  3599.8 1.5 copy-start.11
  3599.8 1194.2 %reduce-scatter.33.cloned.1.call-start = ((), (), s32[]{:S(2)}) async-start(), calls=%async_computation.39 | async-start | bytes 10321920
  3902.5 1.3 copy-start.13
  3902.5 970.2 %reduce-scatter.27.cloned.1.call-start = ((), (), s32[]{:S(2)}) async-start(), calls=%async_computation.31 | async-start | bytes 10321920 | tf_op jit(solution)/shard_map/reduce_scatter | solution.py:311
  4169.6 782.1 %reduce-scatter.29.cloned.1.call-start = ((), (), s32[]{:S(2)}) async-start(), calls=%async_computation.33 | async-start | bytes 10321920 | tf_op jit(solution)/shard_map/reduce_scatter | solution.py:314
  4423.0 31.3 copy-start.33
Sparse Core Ops, SparseCore 0:
  9.6 68.3 all-gather.23
  79.5 64.2 all-gather.21
  146.0 31.4 all-gather.49
  179.5 31.6 all-gather.47
  212.6 225.7 all-gather.25
  439.9 224.9 all-gather.27
  666.5 612.5 all-gather.29
  1280.6 1213.6 all-gather.31
  2495.9 612.6 all-gather.33
  3158.7 50.8 reduce-scatter.16
  3222.9 50.5 reduce-scatter.14
  3275.0 126.6 all-gather.39
  3403.8 56.0 all-gather.51
  3461.9 31.8 all-gather.37
  3495.7 96.2 all-gather.35
  3593.4 278.6 all-gather.45
  3873.5 278.6 all-gather.41
  4153.6 250.6 all-gather.43
  4407.1 133.4 reduce-scatter.30
  4544.3 42.8 reduce-scatter.24
  4591.4 34.4 reduce-scatter.22
  4629.8 34.4 reduce-scatter.20
  4668.1 46.8 reduce-scatter.18
  4718.9 75.0 reduce-scatter.32
  4797.7 75.0 reduce-scatter.26
  4876.6 75.0 reduce-scatter.28
